TPU v7x, 32 devices: a whole 2x2x4 slice. The times are simulated.
32 devices in a mesh: space: 16 (over z, y, core), harm: 2 (over x).
Axes of the slice: x: 2, y: 2, z: 4, core: 2. Of those that a mesh axis runs over, the one named last changes fastest.
Arguments:
- coeffs: bfloat16 [120, 16, 256, 256], P('harm', 'space'), may hold values from -6 to 6
- synthesis: bfloat16 [256, 120], replicated, may hold values from -0.5 to 0.5
- projection: bfloat16 [120, 256], replicated, may hold values from -0.375 to 0.375
- turn_projection: bfloat16 [3, 120, 256], replicated, may hold values from -0.375 to 0.375
- damping: float32 [120], replicated, may hold values from 0.2 to 2
Outputs:
- rate: bfloat16 [120, 16, 256, 256], P('harm', 'space')
- velocity: float32 [3, 16, 256, 256], P(None, 'space', 'harm')
All inputs are finite; a program needn't handle non-finite values.
Results may differ from a plain program's by a relative error of at most 0.0042.
Values may be sent and summed in bfloat16 or wider, within the bound.
A program may use at most 192 MiB of HBM per device.

v0:
```python
import math

import jax
import jax.numpy as jnp
from jax import lax
from jax.sharding import PartitionSpec as P

activity = -3.0
swim_speed = 1.0
transl_diff = 0.25
shape_factor = 0.9
golden_angle = math.pi * (3.0 - math.sqrt(5.0))
stress_pairs = ((0, 3, 4), (3, 1, 5), (4, 5, 2))


def with_halo(cells, sides, width):
    for axis, dim in sides:
        count = lax.axis_size(axis)
        head = lax.slice_in_dim(cells, 0, width, axis=dim)
        tail = lax.slice_in_dim(cells, cells.shape[dim] - width, cells.shape[dim], axis=dim)
        cells = jnp.concatenate(
            [
                lax.ppermute(tail, axis, [(i, (i + 1) % count) for i in range(count)]),
                cells,
                lax.ppermute(head, axis, [((i + 1) % count, i) for i in range(count)]),
            ],
            axis=dim,
        )
    return cells


def sphere_directions(count):
    position = jnp.arange(count, dtype=jnp.float32)
    height = 1.0 - (2.0 * position + 1.0) / count
    radius = jnp.sqrt(1.0 - height * height)
    turning = position * golden_angle
    return jnp.stack([radius * jnp.cos(turning), radius * jnp.sin(turning), height])


def moment_table(synthesis, directions):
    dir_x, dir_y, dir_z = (directions[0], directions[1], directions[2])
    third = 1.0 / 3.0
    moments = jnp.stack(
        [
            dir_x * dir_x - third,
            dir_y * dir_y - third,
            dir_z * dir_z - third,
            dir_x * dir_y,
            dir_x * dir_z,
            dir_y * dir_z,
        ]
    )
    table = jnp.dot(moments, synthesis.astype(jnp.float32), precision=lax.Precision.HIGHEST)
    return (table * (activity / math.sqrt(synthesis.shape[0]))).astype(jnp.bfloat16)


def signed_wave(position, length):
    signed = jnp.where(position < length // 2, position, position - length)
    signed = jnp.where(position == length // 2, 0, signed)
    return 2.0 * math.pi / length * signed.astype(jnp.float32)


def dft_tables(length, frequency):
    phase = jnp.arange(length, dtype=jnp.int32)[:, None] * frequency[None, :] % length
    angle = phase.astype(jnp.float32) * (2.0 * math.pi / length)
    return (jnp.cos(angle), jnp.sin(angle))


def differences(center, lower_z, upper_z, lower_y, upper_y):
    middle = center.astype(jnp.float32)
    upper_x = jnp.roll(middle, -1, 3)
    lower_x = jnp.roll(middle, 1, 3)
    lower_y = lower_y.astype(jnp.float32)
    upper_y = upper_y.astype(jnp.float32)
    lower_z = lower_z.astype(jnp.float32)
    upper_z = upper_z.astype(jnp.float32)
    gradients = (
        (0.5 * (upper_x - lower_x)).astype(jnp.bfloat16),
        (0.5 * (upper_y - lower_y)).astype(jnp.bfloat16),
        (0.5 * (upper_z - lower_z)).astype(jnp.bfloat16),
    )
    laplacian = (upper_x + lower_x + upper_y + lower_y + upper_z + lower_z - 6.0 * middle).astype(
        jnp.bfloat16
    )
    return (gradients, laplacian)


def orient_rates(
    coef_block,
    gradients,
    laplacian,
    flow,
    directions,
    synthesis,
    projection,
    turn_projection,
    damping,
):
    density = jnp.dot(synthesis, coef_block, preferred_element_type=jnp.float32)
    advection = jnp.zeros_like(density)
    for j in range(3):
        slope = jnp.dot(synthesis, gradients[j], preferred_element_type=jnp.float32)
        advection = advection - (swim_speed * directions[j][:, None] + flow[j][None, :]) * slope
    strained = []
    for i in range(3):
        total = jnp.zeros_like(density)
        for j in range(3):
            forward_term = flow[3 + 3 * i + j]
            mirror_term = flow[3 + 3 * j + i]
            coupling = 0.5 * shape_factor * (forward_term + mirror_term) + 0.5 * (
                forward_term - mirror_term
            )
            total = total + coupling[None, :] * directions[j][:, None]
        strained.append(total)
    radial = (
        directions[0][:, None] * strained[0]
        + directions[1][:, None] * strained[1]
        + directions[2][:, None] * strained[2]
    )
    result = jnp.dot(projection, advection.astype(jnp.bfloat16), preferred_element_type=jnp.float32)
    for k in range(3):
        twist = ((strained[k] - directions[k][:, None] * radial) * density).astype(jnp.bfloat16)
        result = result + jnp.dot(turn_projection[k], twist, preferred_element_type=jnp.float32)
    result = (
        result
        + transl_diff * laplacian.astype(jnp.float32)
        - damping[:, None] * coef_block.astype(jnp.float32)
    )
    return result.astype(jnp.bfloat16)


def cell_rates(
    flat_coefs,
    flat_grads,
    flat_lap,
    flat_flow,
    directions,
    synthesis,
    projection,
    turn_projection,
    damping,
):
    cell_count = flat_coefs.shape[1]
    block_len = min(2048, cell_count)

    def advance(block_index, rate_cells):
        offset = block_index * block_len

        def window(array):
            return lax.dynamic_slice_in_dim(array, offset, block_len, 1)

        result = orient_rates(
            window(flat_coefs),
            tuple((window(g) for g in flat_grads)),
            window(flat_lap),
            window(flat_flow),
            directions,
            synthesis,
            projection,
            turn_projection,
            damping,
        )
        return lax.dynamic_update_slice_in_dim(rate_cells, result, offset, 1)

    empty = jnp.zeros(flat_coefs.shape, jnp.bfloat16)
    return lax.fori_loop(0, cell_count // block_len, advance, empty)


def stokes_fields(stress, spaces, groups, space_id, group_id):
    highest = lax.Precision.HIGHEST
    length_x = stress.shape[3]
    cos_x, sin_x = dft_tables(length_x, jnp.arange(length_x, dtype=jnp.int32))
    real_part = jnp.einsum("abcn,nm->ambc", stress, cos_x, precision=highest)
    imag_part = -jnp.einsum("abcn,nm->ambc", stress, sin_x, precision=highest)
    columns = lax.all_to_all(
        lax.all_to_all(
            jnp.stack([real_part, imag_part]), "space", split_axis=2, concat_axis=3, tiled=True
        ),
        "harm",
        split_axis=2,
        concat_axis=4,
        tiled=True,
    )
    real_part, imag_part = (columns[0], columns[1])
    columns_dev = columns.shape[2]
    length_z = columns.shape[3]
    length_y = columns.shape[4]
    cos_y, sin_y = dft_tables(length_y, jnp.arange(length_y, dtype=jnp.int32))
    cos_z, sin_z = dft_tables(length_z, jnp.arange(length_z, dtype=jnp.int32))
    real_next = jnp.einsum("ajzn,nm->ajzm", real_part, cos_y, precision=highest) + jnp.einsum(
        "ajzn,nm->ajzm", imag_part, sin_y, precision=highest
    )
    imag_next = jnp.einsum("ajzn,nm->ajzm", imag_part, cos_y, precision=highest) - jnp.einsum(
        "ajzn,nm->ajzm", real_part, sin_y, precision=highest
    )
    real_part = jnp.einsum("ajny,nm->ajmy", real_next, cos_z, precision=highest) + jnp.einsum(
        "ajny,nm->ajmy", imag_next, sin_z, precision=highest
    )
    imag_part = jnp.einsum("ajny,nm->ajmy", imag_next, cos_z, precision=highest) - jnp.einsum(
        "ajny,nm->ajmy", real_next, sin_z, precision=highest
    )
    column_freq = (
        space_id * groups * columns_dev
        + group_id * columns_dev
        + jnp.arange(columns_dev, dtype=jnp.int32)
    )
    wave_x = signed_wave(column_freq, length_x)[:, None, None]
    wave_y = signed_wave(jnp.arange(length_y, dtype=jnp.int32), length_y)[None, None, :]
    wave_z = signed_wave(jnp.arange(length_z, dtype=jnp.int32), length_z)[None, :, None]
    wave_vec = (wave_x, wave_y, wave_z)
    wave_sq = wave_x * wave_x + wave_y * wave_y + wave_z * wave_z
    inverse = jnp.where(wave_sq > 0, 1.0 / jnp.where(wave_sq > 0, wave_sq, 1.0), 0.0)
    force_real = []
    force_imag = []
    for i in range(3):
        sum_real = (
            real_part[stress_pairs[i][0]] * wave_vec[0]
            + real_part[stress_pairs[i][1]] * wave_vec[1]
            + real_part[stress_pairs[i][2]] * wave_vec[2]
        )
        sum_imag = (
            imag_part[stress_pairs[i][0]] * wave_vec[0]
            + imag_part[stress_pairs[i][1]] * wave_vec[1]
            + imag_part[stress_pairs[i][2]] * wave_vec[2]
        )
        force_real.append(-sum_imag)
        force_imag.append(sum_real)
    along_real = (
        wave_vec[0] * force_real[0] + wave_vec[1] * force_real[1] + wave_vec[2] * force_real[2]
    )
    along_imag = (
        wave_vec[0] * force_imag[0] + wave_vec[1] * force_imag[1] + wave_vec[2] * force_imag[2]
    )
    flow_real = [(force_real[i] - wave_vec[i] * along_real * inverse) * inverse for i in range(3)]
    flow_imag = [(force_imag[i] - wave_vec[i] * along_imag * inverse) * inverse for i in range(3)]
    pieces_real = list(flow_real)
    pieces_imag = list(flow_imag)
    for i in range(3):
        for j in range(3):
            pieces_real.append(-wave_vec[j] * flow_imag[i])
            pieces_imag.append(wave_vec[j] * flow_real[i])
    real_part = jnp.stack(pieces_real)
    imag_part = jnp.stack(pieces_imag)
    real_next = jnp.einsum("ajny,nm->ajmy", real_part, cos_z, precision=highest) - jnp.einsum(
        "ajny,nm->ajmy", imag_part, sin_z, precision=highest
    )
    imag_next = jnp.einsum("ajny,nm->ajmy", imag_part, cos_z, precision=highest) + jnp.einsum(
        "ajny,nm->ajmy", real_part, sin_z, precision=highest
    )
    real_part = jnp.einsum("ajzn,nm->ajzm", real_next, cos_y, precision=highest) - jnp.einsum(
        "ajzn,nm->ajzm", imag_next, sin_y, precision=highest
    )
    imag_part = jnp.einsum("ajzn,nm->ajzm", imag_next, cos_y, precision=highest) + jnp.einsum(
        "ajzn,nm->ajzm", real_next, sin_y, precision=highest
    )
    returned = lax.all_to_all(
        lax.all_to_all(
            jnp.stack([real_part, imag_part]), "space", split_axis=3, concat_axis=2, tiled=True
        ),
        "harm",
        split_axis=4,
        concat_axis=2,
        tiled=True,
    )
    position = jnp.arange(length_x, dtype=jnp.int32)
    owner_group = position // (spaces * columns_dev)
    owner_space = position // columns_dev % spaces
    owner_column = position % columns_dev
    return_freq = owner_space * groups * columns_dev + owner_group * columns_dev + owner_column
    cos_back, sin_back = dft_tables(length_x, return_freq)
    fields = jnp.einsum("akbc,nk->abcn", returned[0], cos_back, precision=highest) - jnp.einsum(
        "akbc,nk->abcn", returned[1], sin_back, precision=highest
    )
    return fields * (1.0 / (length_x * length_y * length_z))


def local(coeffs, synthesis, projection, turn_projection, damping):
    spaces = lax.axis_size("space")
    groups = lax.axis_size("harm")
    space_id = lax.axis_index("space")
    group_id = lax.axis_index("harm")
    local_coefs, planes, length_y, length_x = coeffs.shape
    total_coefs = synthesis.shape[1]
    directions = sphere_directions(synthesis.shape[0])
    table = moment_table(synthesis, directions)
    regrouped = lax.all_to_all(coeffs, "harm", split_axis=2, concat_axis=0, tiled=True)
    padded = with_halo(regrouped, (("space", 1), ("harm", 2)), 1)
    gradients, laplacian = differences(
        regrouped,
        padded[:, :-2, 1:-1],
        padded[:, 2:, 1:-1],
        padded[:, 1:-1, :-2],
        padded[:, 1:-1, 2:],
    )
    cell_shape = regrouped.shape
    own_table = lax.dynamic_slice_in_dim(table, group_id * local_coefs, local_coefs, 1)
    partial_stress = jnp.dot(
        own_table, coeffs.reshape(local_coefs, -1), preferred_element_type=jnp.float32
    )
    partial_stress = partial_stress.reshape(6, planes, length_y, length_x)
    stress = lax.psum_scatter(partial_stress, "harm", scatter_dimension=2, tiled=True)
    fields = stokes_fields(stress, spaces, groups, space_id, group_id)
    rate_cells = cell_rates(
        regrouped.reshape(total_coefs, -1),
        tuple((g.reshape(total_coefs, -1) for g in gradients)),
        laplacian.reshape(total_coefs, -1),
        fields.reshape(12, -1),
        directions,
        synthesis,
        projection,
        turn_projection,
        damping,
    )
    rate = lax.all_to_all(
        rate_cells.reshape(cell_shape), "harm", split_axis=0, concat_axis=2, tiled=True
    )
    return (rate, fields[0:3])


def solution(mesh):
    in_specs = (P("harm", "space", None, None), P(), P(), P(), P())
    out_specs = (P("harm", "space", None, None), P(None, "space", "harm", None))
    return jax.shard_map(local, mesh=mesh, in_specs=in_specs, out_specs=out_specs, check_vma=False)
```

profile of v0, /device:TPU:12, one launch (start us, length us, event | category | flops | bytes accessed | tf_op | source)
XLA Modules:
  0.0 967.8 jit_solution(9093468192187802681)
XLA Ops:
  7.2 11.0 %copy.114 = bf16[60,1,256,256]{3,0,1,2:T(8,128)(2,1)} copy(bf16[60,1,256,256]{3,2,1,0:T(8,128)(2,1)} %param.7) | data formatting | bytes 15728640 | tf_op args[0]
  18.2 7.0 all-to-all-start.4
  25.6 7.4 slice_bitcast_fusion
  33.2 8.9 fusion.72
  42.1 56.2 %reduce-scatter.2.cloned.1.call-done = f32[6,1,128,256]{3,0,2,1:T(8,128)} async-done(((f32[6,1,256,256]{3,0,2,1:T(8,128)}), f32[6,1,128,256]{3,0,2,1:T(8,128)}) %reduce-scatter.2.cloned.1.call-update) | async-done | bytes 786448 | tf_op jit(solution)/shard_map/reduce_scatter | solution.py:301
  108.0 32.2 %all-to-all-done.4 = bf16[60,1,256,256]{3,0,1,2:T(8,128)(2,1)} async-done(((bf16[60,1,256,256]{3,0,1,2:T(8,128)(2,1)}), bf16[60,1,256,256]{3,0,1,2:T(8,128)(2,1)}, u32[]{:S(2)}, u32[]{:S(2)}) %all-to-all-start.4) | async-done | bytes 7864352 | tf_op jit(solution)/shard_map/all_to_all | solution.py:286
  147.2 7.9 copy.115
  160.6 106.7 %all-to-all-done = f32[2,6,256,1,128]{4,0,3,1,2:T(2,128)} async-done(((f32[2,6,256,1,128]{4,0,3,1,2:T(2,128)}), f32[2,6,256,1,128]{4,0,3,1,2:T(2,128)}, u32[]{:S(2)}, u32[]{:S(2)}) %all-to-all-start) | async-done | bytes 1572896 | tf_op jit(solution)/shard_map/all_to_all | solution.py:176
  274.4 17.7 %fusion.293 = (f32[120,1,128,255]{3,2,0,1:T(8,128)}, f32[120,1,128,255]{3,2,0,1:T(8,128)}) fusion(bf16[120,1,128,256]{3,2,0,1:T(8,128)(2,1)} %bitcast.45), kind=kLoop, calls=%fused_computation.404 | loop fusion | bytes 62668800 | tf_op jit(solution)/shard_map/jit(_roll_static)/slice | solution.py:71
  292.1 11.7 %copy.135 = bf16[15,8,128,256]{3,1,2,0:T(8,128)(2,1)} copy(bf16[15,8,128,256]{3,2,1,0:T(8,128)(2,1)} %bitcast.111) | data formatting | bytes 15728640
  303.8 10.3 %fusion.294 = (f32[120,1,128,1]{3,2,0,1:T(8,128)}, f32[120,1,128,1]{3,2,0,1:T(8,128)}) fusion(bf16[120,1,128,256]{3,2,0,1:T(8,128)(2,1)} %bitcast.45), kind=kLoop, calls=%fused_computation.405 | loop fusion | bytes 245760 | tf_op jit(solution)/shard_map/jit(_roll_static)/slice | solution.py:71
  359.5 7.6 collective-permute-done.3
  367.1 46.9 %fusion.69 = (bf16[120,1,128,256]{3,2,0,1:T(8,128)(2,1)}, bf16[120,1,128,256]{3,2,0,1:T(8,128)(2,1)}, bf16[120,1,128,256]{3,2,0,1:T(8,128)(2,1)}) fusion(bf16[120,1,128,256]{3,2,0,1:T(8,128)(2,1)} %collective-permute-done, bf16[120,1,128,256]{3,2,0,1:T(8,128)(2,1)} %collective-permute-done.1, f32[120,1,128,255]{3,2,0,1:T(8,128)} %get-tuple-element.444, ...), kind=kLoop, calls=%fused_computation.100 | loop fusion | flops 137625600 | bytes 79011840 | tf_op jit(solution)/shard_map/convert_element_type | solution.py:82
  414.1 11.7 %copy.132 = bf16[15,8,128,256]{3,1,2,0:T(8,128)(2,1)} copy(bf16[15,8,128,256]{3,2,1,0:T(8,128)(2,1)} %bitcast.307) | data formatting | bytes 15728640
  425.8 11.9 %copy.134 = bf16[15,8,128,256]{3,1,2,0:T(8,128)(2,1)} copy(bf16[15,8,128,256]{3,2,1,0:T(8,128)(2,1)} %bitcast.306) | data formatting | bytes 15728640
  437.7 9.0 copy.136
  457.8 12.7 %fusion.65 = bf16[120,1,128,256]{3,2,0,1:T(8,128)(2,1)S(1)} fusion(bf16[120,3,1,256]{3,2,0,1:T(2,128)(2,1)S(1)} %collective-permute-done.2, bf16[120,1,128,256]{3,2,0,1:T(8,128)(2,1)} %collective-permute-done.1, bf16[120,1,128,256]{3,2,0,1:T(8,128)(2,1)} %bitcast.45, bf16[120,1,128,256]{3,2,0,1:T(8,128)(2,1)} %collective-permute-done, ...), kind=kLoop, calls=%fused_computation.96 | loop fusion | flops 74711040 | bytes 31825920 | tf_op jit(solution)/shard_map/convert_element_type | solution.py:79
  470.5 8.6 copy.133
  479.1 15.2 %all-to-all-done.3 = f32[2,12,128,1,256]{2,0,3,1,4:T(2,128)} async-done(((f32[2,12,128,1,256]{2,0,3,1,4:T(2,128)}), f32[2,12,128,1,256]{2,0,3,1,4:T(2,128)}, u32[]{:S(2)}, u32[]{:S(2)}) %all-to-all-start.3) | async-done | bytes 3145760 | tf_op jit(solution)/shard_map/all_to_all | solution.py:256
  518.7 332.7 %while.15 = (s32[]{:T(128)}, bf16[120,32768]{1,0:T(8,128)(2,1)}, f32[12,32768]{1,0:T(8,128)S(1)}, bf16[120,32768]{1,0:T(8,128)(2,1)}, bf16[256,120]{0,1:T(8,128)...) while((s32[]{:T(128)}, bf16[120,32768]{1,0:T(8,128)(2,1)}, ...), condition=%wide.region_2.3_spmd.clone.clone, body=%wide.region_1.2_spmd.clone.clone.sunk | while | flops 1052165376 | bytes 39649304 | solution.py:166
  851.4 8.7 copy.137
  860.0 6.8 all-to-all-start.5
  868.6 84.4 %all-to-all-done.5 = bf16[120,1,128,256]{3,2,1,0:T(8,128)(2,1)} async-done(((bf16[120,1,128,256]{3,2,1,0:T(8,128)(2,1)}), bf16[120,1,128,256]{3,2,1,0:T(8,128)(2,1)}, u32[]{:S(2)}, u32[]{:S(2)}) %all-to-all-start.5) | async-done | bytes 7864352 | tf_op jit(solution)/shard_map/all_to_all | solution.py:314
  953.1 7.5 copy.118
  (338 shorter events, 443.8 us)
Async XLA Ops:
  18.2 122.1 %all-to-all-start.4 = ((bf16[60,1,256,256]{3,0,1,2:T(8,128)(2,1)}), bf16[60,1,256,256]{3,0,1,2:T(8,128)(2,1)}, u32[]{:S(2)}, u32[]{:S(2)}) async-start(bf16[60,1,256,256]{3,0,1,2:T(8,128)(2,1)} %copy.114), calls=%async_computation.5 | async-start | bytes 16777216 | tf_op jit(solution)/shard_map/all_to_all | solution.py:286
  25.2 73.1 %reduce-scatter.2.cloned.1.call-start = ((), (), s32[]{:S(2)}) async-start(), calls=%async_computation.7 | async-start | bytes 3145728 | tf_op jit(solution)/shard_map/reduce_scatter | solution.py:301
  25.6 7.4 copy-start
  140.3 127.0 %all-to-all-start = ((f32[2,6,256,1,128]{4,0,3,1,2:T(2,128)}), f32[2,6,256,1,128]{4,0,3,1,2:T(2,128)}, u32[]{:S(2)}, u32[]{:S(2)}) async-start(f32[2,6,256,1,128]{4,0,3,1,2:T(2,128)} %copy.105), calls=%async_computation.1 | async-start | bytes 3145728 | tf_op jit(solution)/shard_map/all_to_all | solution.py:176
  158.8 186.8 %collective-permute-start = (bf16[120,1,128,256]{3,2,0,1:T(8,128)(2,1)}, bf16[120,1,128,256]{3,2,0,1:T(8,128)(2,1)}, u32[]{:S(2)}, u32[]{:S(2)}) collective-permute-start(bf16[120,1,128,256]{3,2,0,1:T(8,128)(2,1)} %bitcast.45), channel_id=1, source_target_pairs={{0,2},{2,4},{4,6},{6,8},{8,10},{10,12},{12,14},{14,16},{16,18},{18... | collective-permute-start | bytes 23592968 | tf_op jit(solution)/shard_map/ppermute | solution.py:23
  159.0 186.7 %collective-permute-start.1 = (bf16[120,1,128,256]{3,2,0,1:T(8,128)(2,1)}, bf16[120,1,128,256]{3,2,0,1:T(8,128)(2,1)}, u32[]{:S(2)}, u32[]{:S(2)}) collective-permute-start(bf16[120,1,128,256]{3,2,0,1:T(8,128)(2,1)} %bitcast.45), channel_id=1, source_target_pairs={{2,0},{4,2},{6,4},{8,6},{10,8},{12,10},{14,12},{16,14},{18,16},{20... | collective-permute-start | bytes 23592968 | tf_op jit(solution)/shard_map/ppermute | solution.py:25
  270.7 43.4 %all-to-all-start.1 = ((f32[2,6,16,16,128]{4,3,1,0,2:T(8,128)}), f32[2,6,16,16,128]{4,3,1,0,2:T(8,128)S(1)}, u32[]{:S(2)}, u32[]{:S(2)}) async-start(f32[2,6,16,16,128]{4,3,1,0,2:T(8,128)} %bitcast.248), calls=%async_computation.2 | async-start | bytes 3145728 | tf_op jit(solution)/shard_map/all_to_all | solution.py:175
  348.0 11.5 %collective-permute-start.2 = (bf16[120,3,1,256]{3,2,0,1:T(2,128)(2,1)S(1)}, bf16[120,3,1,256]{3,2,0,1:T(2,128)(2,1)S(1)}, u32[]{:S(2)}, u32[]{:S(2)}) collective-permute-start(bf16[120,3,1,256]{3,2,0,1:T(2,128)(2,1)S(1)} %get-tuple-element.441), channel_id=1, source_target_pairs={{1,0},{0,1},{3,2},{2,3},{5,4},{4,5},{7,6},{6,7},{9,8},{8,9},{11,10... | collective-permute-start | bytes 552968 | tf_op jit(solution)/shard_map/ppermute | solution.py:25
  350.1 17.1 %collective-permute-start.3 = (bf16[120,3,1,256]{3,2,0,1:T(2,128)(2,1)S(1)}, bf16[120,3,1,256]{3,2,0,1:T(2,128)(2,1)S(1)}, u32[]{:S(2)}, u32[]{:S(2)}) collective-permute-start(bf16[120,3,1,256]{3,2,0,1:T(2,128)(2,1)S(1)} %get-tuple-element.440), channel_id=1, source_target_pairs={{0,1},{1,0},{2,3},{3,2},{4,5},{5,4},{6,7},{7,6},{8,9},{9,8},{10,11... | collective-permute-start | bytes 552968 | tf_op jit(solution)/shard_map/ppermute | solution.py:23
  354.1 92.6 %all-to-all-start.2 = ((f32[2,12,8,16,256]{4,2,1,0,3:T(8,128)}), f32[2,12,8,16,256]{4,2,1,0,3:T(8,128)}, u32[]{:S(2)}, u32[]{:S(2)}) async-start(f32[2,12,8,16,256]{4,2,1,0,3:T(8,128)} %copy.108), calls=%async_computation.3 | async-start | bytes 6291456 | tf_op jit(solution)/shard_map/all_to_all | solution.py:257
  367.1 47.0 %copy-start.6 = (bf16[120,3,1,256]{3,2,0,1:T(2,128)(2,1)}, bf16[120,3,1,256]{3,2,0,1:T(2,128)(2,1)S(1)}, u32[]{:S(2)}) copy-start(bf16[120,3,1,256]{3,2,0,1:T(2,128)(2,1)S(1)} %collective-permute-done.3) | copy-start | bytes 552964
  425.8 11.9 %slice-start = ((s8[7864320]{0:T(1024)(128)(4,1)}), s8[4194304]{0:T(1024)(128)(4,1)S(1)}, s32[]{:S(2)}) async-start(s8[7864320]{0:T(1024)(128)(4,1)} %bitcast.303), calls=%async_computation.8 | async-start | bytes 8388608
  425.8 11.9 %slice-start.1 = ((s8[7864320]{0:T(1024)(128)(4,1)}), s8[3670016]{0:T(1024)(128)(4,1)S(1)}, s32[]{:S(2)}) async-start(s8[7864320]{0:T(1024)(128)(4,1)} %bitcast.303), calls=%async_computation.9 | async-start | bytes 7340032
  452.5 41.9 %all-to-all-start.3 = ((f32[2,12,128,1,256]{2,0,3,1,4:T(2,128)}), f32[2,12,128,1,256]{2,0,3,1,4:T(2,128)}, u32[]{:S(2)}, u32[]{:S(2)}) async-start(f32[2,12,128,1,256]{2,0,3,1,4:T(2,128)} %copy.110), calls=%async_computation.4 | async-start | bytes 6291456 | tf_op jit(solution)/shard_map/all_to_all | solution.py:256
  555.1 5.4 copy-start.4
  575.9 5.4 copy-start.4
  596.7 5.4 copy-start.4
  617.5 5.4 copy-start.4
  638.2 5.4 copy-start.4
  659.0 5.4 copy-start.4
  679.8 5.4 copy-start.4
  742.1 5.4 copy-start.4
  762.9 5.4 copy-start.4
  860.0 93.0 %all-to-all-start.5 = ((bf16[120,1,128,256]{3,2,1,0:T(8,128)(2,1)}), bf16[120,1,128,256]{3,2,1,0:T(8,128)(2,1)}, u32[]{:S(2)}, u32[]{:S(2)}) async-start(bf16[120,1,128,256]{3,2,1,0:T(8,128)(2,1)} %bitcast.301), calls=%async_computation.6 | async-start | bytes 15728640 | tf_op jit(solution)/shard_map/all_to_all | solution.py:314
  (29 other events, 82.2 us)
Sparse Core Ops, SparseCore 0:
  42.2 56.0 reduce-scatter.1
where the time goes:
time: 977 us; the launch traced here: 968 us
  matrix products  358 us (37%)
  waiting for transfers between devices  303 us (31%)
  local copies, waits for them, and re-layouts  183 us (19%)
  other arithmetic  69.8 us (7%)
  starting transfers between devices  38.8 us (4%)
  between operations  15.1 us (2%)
    dot_general x48, matrix products, orient_rates(): jnp.dot(turn_projection[k], twist, preferred_element_type=jnp.float32)  172 us
    all_to_all x1, waiting for transfers between devices, stokes_fields(): lax.all_to_all(jnp.stack([real_part, imag_part]), 'space', split_axis=2,...  107 us
    all_to_all x1, waiting for transfers between devices, local(): lax.all_to_all(rate_cells.reshape(cell_shape), 'harm', split_axis=0, conc...  84.4 us
    unnamed x30, local copies, waits for them, and re-layouts  77 us
    dot_general x32, matrix products, orient_rates(): slope = jnp.dot(synthesis, gradients[j], preferred_element_type=jnp.float32)  71.4 us
    reduce_scatter x1, waiting for transfers between devices, local(): lax.psum_scatter(partial_stress, 'harm', scatter_dimension=2, tiled=True)  56.2 us
    convert_element_type x1, other arithmetic, differences(): (upper_x + lower_x + upper_y + lower_y + upper_z + lower_z - 6.0 * middle...  46.9 us
    dot_general x16, matrix products, orient_rates(): jnp.dot(projection, advection.astype(jnp.bfloat16), preferred_element_typ...  42.3 us
  transfers between devices with their start and end apart: 11, of which 7 were waited for; matrix products, arithmetic and copies ran while one was open for 23% of the time, Pallas kernels for 0%

commit v1 on v0

--- a/solution.py
+++ b/solution.py
@@ -85,61 +85,50 @@
     return (gradients, laplacian)
 
 
-def orient_rates(
-    coef_block,
-    gradients,
-    laplacian,
-    flow,
-    directions,
-    synthesis,
-    projection,
-    turn_projection,
-    damping,
-):
-    density = jnp.dot(synthesis, coef_block, preferred_element_type=jnp.float32)
-    advection = jnp.zeros_like(density)
-    for j in range(3):
-        slope = jnp.dot(synthesis, gradients[j], preferred_element_type=jnp.float32)
-        advection = advection - (swim_speed * directions[j][:, None] + flow[j][None, :]) * slope
-    strained = []
+def composite_tables(directions, synthesis, projection, turn_projection):
+    def through(weights):
+        return jnp.dot(weights, synthesis.astype(jnp.float32), precision=lax.Precision.HIGHEST)
+
+    project = projection.astype(jnp.float32)
+    turning = turn_projection.astype(jnp.float32)
+    radial = sum(turning[k] * directions[k] for k in range(3))
+    tables = [through(-swim_speed * project * directions[j]) for j in range(3)]
+    tables.append(through(-project))
+    strain = [
+        [through((turning[i] - radial * directions[i]) * directions[j]) for j in range(3)]
+        for i in range(3)
+    ]
     for i in range(3):
-        total = jnp.zeros_like(density)
         for j in range(3):
-            forward_term = flow[3 + 3 * i + j]
-            mirror_term = flow[3 + 3 * j + i]
-            coupling = 0.5 * shape_factor * (forward_term + mirror_term) + 0.5 * (
-                forward_term - mirror_term
-            )
-            total = total + coupling[None, :] * directions[j][:, None]
-        strained.append(total)
-    radial = (
-        directions[0][:, None] * strained[0]
-        + directions[1][:, None] * strained[1]
-        + directions[2][:, None] * strained[2]
-    )
-    result = jnp.dot(projection, advection.astype(jnp.bfloat16), preferred_element_type=jnp.float32)
-    for k in range(3):
-        twist = ((strained[k] - directions[k][:, None] * radial) * density).astype(jnp.bfloat16)
-        result = result + jnp.dot(turn_projection[k], twist, preferred_element_type=jnp.float32)
-    result = (
-        result
-        + transl_diff * laplacian.astype(jnp.float32)
-        - damping[:, None] * coef_block.astype(jnp.float32)
-    )
+            if i + j < 4:
+                tables.append(strain[i][j] - strain[2][2] if i == j else strain[i][j])
+    stacked = jnp.stack(tables, axis=1)
+    coefs = stacked.shape[2]
+    stacked = jnp.pad(stacked, ((0, 0), (0, 0), (0, -coefs % 16)))
+    return stacked.astype(jnp.bfloat16).reshape(stacked.shape[0], -1)
+
+
+def orient_rates(coef_block, gradients, laplacian, flow, tables, damping):
+    middle = coef_block.astype(jnp.float32)
+    carried = sum(flow[j][None, :] * gradients[j].astype(jnp.float32) for j in range(3))
+    inputs = [*gradients, carried.astype(jnp.bfloat16)]
+    for i in range(3):
+        for j in range(3):
+            if i + j < 4:
+                forward_term = flow[3 + 3 * i + j]
+                mirror_term = flow[3 + 3 * j + i]
+                coupling = 0.5 * shape_factor * (forward_term + mirror_term) + 0.5 * (
+                    forward_term - mirror_term
+                )
+                inputs.append((coupling[None, :] * middle).astype(jnp.bfloat16))
+    extra = -coef_block.shape[0] % 16
+    inputs = jnp.concatenate([jnp.pad(x, ((0, extra), (0, 0))) for x in inputs], axis=0)
+    result = jnp.dot(tables, inputs, preferred_element_type=jnp.float32)
+    result = result + transl_diff * laplacian.astype(jnp.float32) - damping[:, None] * middle
     return result.astype(jnp.bfloat16)
 
 
-def cell_rates(
-    flat_coefs,
-    flat_grads,
-    flat_lap,
-    flat_flow,
-    directions,
-    synthesis,
-    projection,
-    turn_projection,
-    damping,
-):
+def cell_rates(flat_coefs, flat_grads, flat_lap, flat_flow, tables, damping):
     cell_count = flat_coefs.shape[1]
     block_len = min(2048, cell_count)
 
@@ -154,10 +143,7 @@
             tuple((window(g) for g in flat_grads)),
             window(flat_lap),
             window(flat_flow),
-            directions,
-            synthesis,
-            projection,
-            turn_projection,
+            tables,
             damping,
         )
         return lax.dynamic_update_slice_in_dim(rate_cells, result, offset, 1)
@@ -167,20 +153,27 @@
 
 
 def stokes_fields(stress, spaces, groups, space_id, group_id):
-    highest = lax.Precision.HIGHEST
+    highest = lax.Precision.HIGH
     length_x = stress.shape[3]
-    cos_x, sin_x = dft_tables(length_x, jnp.arange(length_x, dtype=jnp.int32))
+    packed = (length_x // 2) % (spaces * groups) == 0
+    slots = length_x // 2 if packed else length_x
+    cos_x, sin_x = dft_tables(length_x, jnp.arange(slots, dtype=jnp.int32))
+    parity = 1.0 - 2.0 * (jnp.arange(length_x, dtype=jnp.int32) % 2).astype(jnp.float32)
+    sin_x = -sin_x
+    if packed:
+        sin_x = sin_x.at[:, 0].set(parity)
     real_part = jnp.einsum("abcn,nm->ambc", stress, cos_x, precision=highest)
-    imag_part = -jnp.einsum("abcn,nm->ambc", stress, sin_x, precision=highest)
+    imag_part = jnp.einsum("abcn,nm->ambc", stress, sin_x, precision=highest)
     columns = lax.all_to_all(
         lax.all_to_all(
-            jnp.stack([real_part, imag_part]), "space", split_axis=2, concat_axis=3, tiled=True
+            jnp.stack([real_part, imag_part]).astype(jnp.bfloat16), "space", split_axis=2, concat_axis=3, tiled=True
         ),
         "harm",
         split_axis=2,
         concat_axis=4,
         tiled=True,
     )
+    columns = columns.astype(jnp.float32)
     real_part, imag_part = (columns[0], columns[1])
     columns_dev = columns.shape[2]
     length_z = columns.shape[3]
@@ -236,7 +229,7 @@
     pieces_real = list(flow_real)
     pieces_imag = list(flow_imag)
     for i in range(3):
-        for j in range(3):
+        for j in range(1, 3 if i < 2 else 2):
             pieces_real.append(-wave_vec[j] * flow_imag[i])
             pieces_imag.append(wave_vec[j] * flow_real[i])
     real_part = jnp.stack(pieces_real)
@@ -255,23 +248,54 @@
     )
     returned = lax.all_to_all(
         lax.all_to_all(
-            jnp.stack([real_part, imag_part]), "space", split_axis=3, concat_axis=2, tiled=True
+            jnp.stack([real_part, imag_part]).astype(jnp.bfloat16), "space", split_axis=3, concat_axis=2, tiled=True
         ),
         "harm",
         split_axis=4,
         concat_axis=2,
         tiled=True,
     )
-    position = jnp.arange(length_x, dtype=jnp.int32)
+    returned = returned.astype(jnp.float32)
+    position = jnp.arange(slots, dtype=jnp.int32)
     owner_group = position // (spaces * columns_dev)
     owner_space = position // columns_dev % spaces
     owner_column = position % columns_dev
     return_freq = owner_space * groups * columns_dev + owner_group * columns_dev + owner_column
     cos_back, sin_back = dft_tables(length_x, return_freq)
-    fields = jnp.einsum("akbc,nk->abcn", returned[0], cos_back, precision=highest) - jnp.einsum(
-        "akbc,nk->abcn", returned[1], sin_back, precision=highest
-    )
-    return fields * (1.0 / (length_x * length_y * length_z))
+    from_real, from_imag = cos_back, -sin_back
+    if packed:
+        first = (return_freq == 0)[None, :]
+        from_real = jnp.where(first, 1.0, 2.0 * from_real)
+        from_imag = jnp.where(first, parity[:, None], 2.0 * from_imag)
+    scale = 1.0 / (length_x * length_y * length_z)
+    from_real, from_imag = from_real * scale, from_imag * scale
+    wave_back = signed_wave(return_freq, length_x)[None, :]
+
+    def back(pieces_real, pieces_imag, table_real, table_imag):
+        return jnp.einsum("akbc,nk->abcn", pieces_real, table_real, precision=highest) + jnp.einsum(
+            "akbc,nk->abcn", pieces_imag, table_imag, precision=highest
+        )
+
+    plain = back(returned[0], returned[1], from_real, from_imag)
+    along_x = back(returned[0, :3], returned[1, :3], wave_back * from_imag, -wave_back * from_real)
+    velocity, others = plain[:3], plain[3:]
+    trace_rest = -(along_x[0] + others[2])
+    return jnp.stack(
+        [
+            velocity[0],
+            velocity[1],
+            velocity[2],
+            along_x[0],
+            others[0],
+            others[1],
+            along_x[1],
+            others[2],
+            others[3],
+            along_x[2],
+            others[4],
+            trace_rest,
+        ]
+    )
 
 
 def local(coeffs, synthesis, projection, turn_projection, damping):
@@ -305,10 +329,7 @@
         tuple((g.reshape(total_coefs, -1) for g in gradients)),
         laplacian.reshape(total_coefs, -1),
         fields.reshape(12, -1),
-        directions,
-        synthesis,
-        projection,
-        turn_projection,
+        composite_tables(directions, synthesis, projection, turn_projection),
         damping,
     )
     rate = lax.all_to_all(

time: 977 us -> 792 us (0.81)
  matrix products: 358 us -> 82 us
  blocking collectives: 0 us -> 90.9 us
  other arithmetic: 69.8 us -> 139 us
  waiting for transfers between devices: 303 us -> 253 us
  local copies, waits for them, and re-layouts: 183 us -> 165 us
    dot_general x115 -> x34, matrix products: 318 us -> 57.1 us  [the longest x16 48.6 us: orient_rates(): result = jnp.dot(tables, inputs, preferred_element_type=jnp.float32)]
    all_to_all x0 -> x1, blocking collectives: none -> 90.9 us  [local(): lax.all_to_all(rate_cells.reshape(cell_shape), 'harm', split_axis=0, conc...]
    all_to_all x5 -> x4, waiting for transfers between devices: 206 us -> 133 us  [the longest x2 133 us: stokes_fields(): lax.all_to_all(jnp.stack([real_part, imag_part]).astype(jnp.bfloat16), 's...]
    all_to_all x1, waiting for transfers between devices: 32.2 us -> 88.7 us  [local(): lax.all_to_all(coeffs, 'harm', split_axis=2, concat_axis=0, tiled=True)]
    convert_element_type x0 -> x17, other arithmetic: none -> 46.5 us  [the longest x16 46.5 us: orient_rates(): inputs.append((coupling[None, :] * middle).astype(jnp.bfloat16))]
    reduce_scatter x1, waiting for transfers between devices: 56.2 us -> 30.7 us  [local(): lax.psum_scatter(partial_stress, 'harm', scatter_dimension=2, tiled=True)]
    add x16, other arithmetic: 4.18 us -> 25.6 us  [orient_rates(): 0.5 * shape_factor * (forward_term + mirror_term)]
    another operation x5 -> x4, local copies, waits for them, and re-layouts: 17.2 us -> 25 us  [the longest x1 15.4 us: stokes_fields(): jnp.stack([velocity[0], velocity[1], velocity[2], along_x[0], others[0],...]
  transfers between devices with their start and end apart: 11 -> 10, of which waited for: 7 -> 4; matrix products, arithmetic and copies ran while one was open for 23% -> 15% of each run, Pallas kernels for 0% -> 0%
where the time goes in v1:
time: 792 us; the launch traced here: 779 us
  waiting for transfers between devices  253 us (32%)
  local copies, waits for them, and re-layouts  165 us (21%)
  other arithmetic  139 us (18%)
  blocking collectives  90.9 us (11%)
  matrix products  82 us (10%)
  starting transfers between devices  31.8 us (4%)
  between operations  15.2 us (2%)
    all_to_all x2, waiting for transfers between devices, stokes_fields(): lax.all_to_all(jnp.stack([real_part, imag_part]).astype(jnp.bfloat16), 's...  133 us
    all_to_all x1, blocking collectives, local(): lax.all_to_all(rate_cells.reshape(cell_shape), 'harm', split_axis=0, conc...  90.9 us
    all_to_all x1, waiting for transfers between devices, local(): lax.all_to_all(coeffs, 'harm', split_axis=2, concat_axis=0, tiled=True)  88.7 us
    unnamed x36, local copies, waits for them, and re-layouts  74.5 us
    dot_general x16, matrix products, orient_rates(): result = jnp.dot(tables, inputs, preferred_element_type=jnp.float32)  48.6 us
    convert_element_type x1, other arithmetic, differences(): (upper_x + lower_x + upper_y + lower_y + upper_z + lower_z - 6.0 * middle...  47.1 us
    convert_element_type x16, other arithmetic, orient_rates(): inputs.append((coupling[None, :] * middle).astype(jnp.bfloat16))  46.5 us
    reduce_scatter x1, waiting for transfers between devices, local(): lax.psum_scatter(partial_stress, 'harm', scatter_dimension=2, tiled=True)  30.7 us
  transfers between devices with their start and end apart: 10, of which 4 were waited for; matrix products, arithmetic and copies ran while one was open for 15% of the time, Pallas kernels for 0%

profile of v1, /device:TPU:12, one launch (start us, length us, event | category | flops | bytes accessed | tf_op | source)
XLA Modules:
  0.0 778.5 jit_solution(12854564702148232479)
XLA Ops:
  7.4 7.4 slice_bitcast_fusion
  14.9 8.9 %fusion.20 = f32[6,1,256,256]{3,0,2,1:T(8,128)} fusion(bf16[256,256,60]{1,0,2:T(8,128)(2,1)} %slice_bitcast_fusion, bf16[6,120]{1,0:T(8,128)(2,1)S(1)} %fusion.59, s32[]{:T(128)S(6)} %select_n.481), kind=kOutput, calls=%fused_computation.74 | convolution fusion | flops 47185920 | bytes 9438628 | tf_op jit(solution)/shard_map/dot_general | solution.py:321
  26.3 30.7 %reduce-scatter.2.cloned.1.call-done = f32[6,1,128,256]{3,0,2,1:T(8,128)} async-done(((f32[6,1,256,256]{3,0,2,1:T(8,128)}), f32[6,1,128,256]{3,0,2,1:T(8,128)}) %reduce-scatter.2.cloned.1.call-update) | async-done | bytes 786448 | tf_op jit(solution)/shard_map/reduce_scatter | solution.py:325
  62.5 6.3 all-to-all-start.1
  68.9 11.0 %copy.135 = bf16[60,1,256,256]{3,0,1,2:T(8,128)(2,1)} copy(bf16[60,1,256,256]{3,2,1,0:T(8,128)(2,1)} %param.9) | data formatting | bytes 15728640 | tf_op args[0]
  80.7 7.1 all-to-all-start
  91.9 88.7 %all-to-all-done = bf16[60,1,256,256]{3,0,1,2:T(8,128)(2,1)} async-done(((bf16[60,1,256,256]{3,0,1,2:T(8,128)(2,1)}), bf16[60,1,256,256]{3,0,1,2:T(8,128)(2,1)}, u32[]{:S(2)}, u32[]{:S(2)}) %all-to-all-start) | async-done | bytes 7864352 | tf_op jit(solution)/shard_map/all_to_all | solution.py:310
  184.9 7.9 %copy.136 = bf16[60,1,256,256]{3,2,0,1:T(8,128)(2,1)S(1)} copy(bf16[60,1,256,256]{3,0,1,2:T(8,128)(2,1)} %all-to-all-done) | data formatting | bytes 15728640 | tf_op jit(solution)/shard_map/all_to_all | solution.py:310
  216.7 6.5 all-to-all-start.3
  223.2 17.6 %fusion.343 = (f32[120,1,128,255]{3,2,0,1:T(8,128)}, f32[120,1,128,255]{3,2,0,1:T(8,128)}) fusion(bf16[120,1,128,256]{3,2,0,1:T(8,128)(2,1)} %bitcast.14), kind=kLoop, calls=%fused_computation.515 | loop fusion | bytes 62668800 | tf_op jit(solution)/shard_map/jit(_roll_static)/slice | solution.py:71
  240.8 132.7 %all-to-all-done.3 = bf16[2,8,4,16,256]{4,2,1,0,3:T(4,128)(2,1)S(1)} async-done(((bf16[2,8,4,16,256]{4,2,1,0,3:T(4,128)(2,1)}), bf16[2,8,4,16,256]{4,2,1,0,3:T(4,128)(2,1)S(1)}, u32[]{:S(2)}, u32[]{:S(2)}) %all-to-all-start.3) | async-done | bytes 524320 | tf_op jit(solution)/shard_map/all_to_all | solution.py:250
  379.8 10.3 %fusion.344 = (f32[120,1,128,1]{3,2,0,1:T(8,128)}, f32[120,1,128,1]{3,2,0,1:T(8,128)}) fusion(bf16[120,1,128,256]{3,2,0,1:T(8,128)(2,1)} %bitcast.14), kind=kLoop, calls=%fused_computation.516 | loop fusion | bytes 245760 | tf_op jit(solution)/shard_map/jit(_roll_static)/slice | solution.py:71
  390.1 11.7 %copy.190 = bf16[15,8,128,256]{3,1,2,0:T(8,128)(2,1)} copy(bf16[15,8,128,256]{3,2,1,0:T(8,128)(2,1)} %bitcast.138) | data formatting | bytes 15728640
  415.6 15.4 %stack.142 = f32[12,32768]{1,0:T(8,128)} concatenate(f32[3,32768]{1,0:T(4,128)S(1)} %bitcast.373, f32[1,32768]{1,0:T(1,128)S(1)} %bitcast.378, f32[2,32768]{1,0:T(2,128)S(1)} %bitcast.381, f32[1,32768]{1,0:T(1,128)S(1)} %bitcast.397, f32[2,32768]{1,0:T(2,128)S(1)} %bitcast.382, f32[1,32768]{1,0:T(1,128)S(1)} %bitcast.398, f32[1,32768]{1,0:T(1,128)S(1)} %bitcast.399, ...), dimensions={0} | concatenate | bytes 3145728 | tf_op jit(solution)/shard_map/stack | solution.py:283
  432.0 47.1 %fusion.17 = (bf16[120,1,128,256]{3,2,0,1:T(8,128)(2,1)}, bf16[120,1,128,256]{3,2,0,1:T(8,128)(2,1)}, bf16[120,1,128,256]{3,2,0,1:T(8,128)(2,1)}) fusion(bf16[120,1,128,256]{3,2,0,1:T(8,128)(2,1)} %collective-permute-done, bf16[120,1,128,256]{3,2,0,1:T(8,128)(2,1)} %collective-permute-done.1, f32[120,1,128,255]{3,2,0,1:T(8,128)} %get-tuple-element.398, ...), kind=kLoop, calls=%fused_computation.61 | loop fusion | flops 137625600 | bytes 79011840 | tf_op jit(solution)/shard_map/convert_element_type | solution.py:82
  479.1 11.8 %copy.177 = bf16[15,8,128,256]{3,1,2,0:T(8,128)(2,1)} copy(bf16[15,8,128,256]{3,2,1,0:T(8,128)(2,1)} %bitcast.359) | data formatting | bytes 15728640
  490.9 11.8 %copy.179 = bf16[15,8,128,256]{3,1,2,0:T(8,128)(2,1)} copy(bf16[15,8,128,256]{3,2,1,0:T(8,128)(2,1)} %bitcast.358) | data formatting | bytes 15728640
  502.8 8.8 %copy.191 = bf16[15,8,128,256]{3,1,2,0:T(8,128)(2,1)} copy(bf16[15,8,128,256]{3,2,1,0:T(8,128)(2,1)S(1)} %bitcast.357) | data formatting | bytes 15728640
  511.5 12.8 %fusion.13 = bf16[120,1,128,256]{3,2,0,1:T(8,128)(2,1)S(1)} fusion(bf16[120,3,1,256]{3,2,0,1:T(2,128)(2,1)S(1)} %collective-permute-done.2, bf16[120,1,128,256]{3,2,0,1:T(8,128)(2,1)} %collective-permute-done.1, bf16[120,1,128,256]{3,2,0,1:T(8,128)(2,1)} %bitcast.14, bf16[120,1,128,256]{3,2,0,1:T(8,128)(2,1)} %collective-permute-done, ...), kind=kLoop, calls=%fused_computation.57 | loop fusion | flops 74711040 | bytes 31825920 | tf_op jit(solution)/shard_map/convert_element_type | solution.py:79
  524.3 8.6 %copy.178 = bf16[15,8,128,256]{3,1,2,0:T(8,128)(2,1)} copy(bf16[15,8,128,256]{3,2,1,0:T(8,128)(2,1)S(1)} %bitcast.350) | data formatting | bytes 15728640
  537.0 130.3 %while.16 = (s32[]{:T(128)}, bf16[120,32768]{1,0:T(8,128)(2,1)}, bf16[120,32768]{1,0:T(8,128)(2,1)}, bf16[120,32768]{1,0:T(8,128)(2,1)}, bf16[120,32768]{1,0:T(8...) while((s32[]{:T(128)}, bf16[120,32768]{1,0:T(8,128)(2,1)}, ...), condition=%wide.region_3.4_spmd, body=%wide.region_2.3_spmd.sunk | while | flops 763154432 | bytes 28459920 | solution.py:152
  667.2 5.6 copy.192
  672.8 90.9 %all_to_all.105 = bf16[120,1,128,256]{3,2,1,0:T(8,128)(2,1)} all-to-all(bf16[120,1,128,256]{3,2,1,0:T(8,128)(2,1)S(1)} %bitcast.353), channel_id=1, replica_groups=mesh['space'=16,'harm'=2] {'harm'}, dimensions={0} | all-to-all | bytes 15728640 | tf_op jit(solution)/shard_map/all_to_all | solution.py:335
  763.8 7.5 copy.160
  (383 shorter events, 194.5 us)
Async XLA Ops:
  7.2 7.6 copy-start
  7.2 49.8 %reduce-scatter.2.cloned.1.call-start = ((), (), s32[]{:S(2)}) async-start(), calls=%async_computation.7 | async-start | bytes 3145728 | tf_op jit(solution)/shard_map/reduce_scatter | solution.py:325
  62.5 18.1 %all-to-all-start.1 = ((bf16[2,6,128,1,128]{4,0,3,1,2:T(2,128)(2,1)}), bf16[2,6,128,1,128]{4,0,3,1,2:T(2,128)(2,1)S(1)}, u32[]{:S(2)}, u32[]{:S(2)}) async-start(bf16[2,6,128,1,128]{4,0,3,1,2:T(2,128)(2,1)} %copy.143), calls=%async_computation.2 | async-start | bytes 786432 | tf_op jit(solution)/shard_map/all_to_all | solution.py:168
  68.9 11.0 %copy-start.2 = (bf16[120,256]{1,0:T(8,128)(2,1)S(1)}, bf16[120,256]{1,0:T(8,128)(2,1)}, u32[]{:S(2)}) copy-start(bf16[120,256]{1,0:T(8,128)(2,1)} %param.11) | copy-start | bytes 184324
  80.6 7.2 copy-start.3
  80.7 100.0 %all-to-all-start = ((bf16[60,1,256,256]{3,0,1,2:T(8,128)(2,1)}), bf16[60,1,256,256]{3,0,1,2:T(8,128)(2,1)}, u32[]{:S(2)}, u32[]{:S(2)}) async-start(bf16[60,1,256,256]{3,0,1,2:T(8,128)(2,1)} %copy.135), calls=%async_computation | async-start | bytes 16777216 | tf_op jit(solution)/shard_map/all_to_all | solution.py:310
  180.6 18.1 %all-to-all-start.2 = ((bf16[2,6,8,16,128]{4,3,1,0,2:T(8,128)(2,1)}), bf16[2,6,8,16,128]{4,3,1,0,2:T(8,128)(2,1)}, u32[]{:S(2)}, u32[]{:S(2)}) async-start(bf16[2,6,8,16,128]{4,3,1,0,2:T(8,128)(2,1)} %bitcast.321), calls=%async_computation.3 | async-start | bytes 786432 | tf_op jit(solution)/shard_map/all_to_all | solution.py:167
  196.5 213.3 %collective-permute-start = (bf16[120,1,128,256]{3,2,0,1:T(8,128)(2,1)}, bf16[120,1,128,256]{3,2,0,1:T(8,128)(2,1)}, u32[]{:S(2)}, u32[]{:S(2)}) collective-permute-start(bf16[120,1,128,256]{3,2,0,1:T(8,128)(2,1)} %bitcast.14), channel_id=1, source_target_pairs={{0,2},{2,4},{4,6},{6,8},{8,10},{10,12},{12,14},{14,16},{16,18},{18... | collective-permute-start | bytes 23592968 | tf_op jit(solution)/shard_map/ppermute | solution.py:23
  196.5 213.3 %collective-permute-start.1 = (bf16[120,1,128,256]{3,2,0,1:T(8,128)(2,1)}, bf16[120,1,128,256]{3,2,0,1:T(8,128)(2,1)}, u32[]{:S(2)}, u32[]{:S(2)}) collective-permute-start(bf16[120,1,128,256]{3,2,0,1:T(8,128)(2,1)} %bitcast.14), channel_id=1, source_target_pairs={{2,0},{4,2},{6,4},{8,6},{10,8},{12,10},{14,12},{16,14},{18,16},{20... | collective-permute-start | bytes 23592968 | tf_op jit(solution)/shard_map/ppermute | solution.py:25
  216.7 156.8 %all-to-all-start.3 = ((bf16[2,8,4,16,256]{4,2,1,0,3:T(4,128)(2,1)}), bf16[2,8,4,16,256]{4,2,1,0,3:T(4,128)(2,1)S(1)}, u32[]{:S(2)}, u32[]{:S(2)}) async-start(bf16[2,8,4,16,256]{4,2,1,0,3:T(4,128)(2,1)} %copy.146), calls=%async_computation.4 | async-start | bytes 1048576 | tf_op jit(solution)/shard_map/all_to_all | solution.py:250
  376.3 25.5 %all-to-all-start.4 = ((bf16[2,2,65536]{2,1,0:T(2,128)(2,1)}), bf16[2,2,65536]{2,1,0:T(2,128)(2,1)S(1)}, u32[]{:S(2)}, u32[]{:S(2)}) async-start(bf16[2,2,65536]{2,1,0:T(2,128)(2,1)} %reshape.575), calls=%async_computation.5 | async-start | bytes 1048576 | tf_op jit(solution)/shard_map/all_to_all | solution.py:249
  412.9 18.0 %collective-permute-start.2 = (bf16[120,3,1,256]{3,2,0,1:T(2,128)(2,1)}, bf16[120,3,1,256]{3,2,0,1:T(2,128)(2,1)S(1)}, u32[]{:S(2)}, u32[]{:S(2)}) collective-permute-start(bf16[120,3,1,256]{3,2,0,1:T(2,128)(2,1)} %get-tuple-element.395), channel_id=1, source_target_pairs={{1,0},{0,1},{3,2},{2,3},{5,4},{4,5},{7,6},{6,7},{9,8},{8,9},{11,10... | collective-permute-start | bytes 552968 | tf_op jit(solution)/shard_map/ppermute | solution.py:25
  415.0 17.0 %collective-permute-start.3 = (bf16[120,3,1,256]{3,2,0,1:T(2,128)(2,1)S(1)}, bf16[120,3,1,256]{3,2,0,1:T(2,128)(2,1)S(1)}, u32[]{:S(2)}, u32[]{:S(2)}) collective-permute-start(bf16[120,3,1,256]{3,2,0,1:T(2,128)(2,1)S(1)} %get-tuple-element.394), channel_id=1, source_target_pairs={{0,1},{1,0},{2,3},{3,2},{4,5},{5,4},{6,7},{7,6},{8,9},{9,8},{10,11... | collective-permute-start | bytes 552968 | tf_op jit(solution)/shard_map/ppermute | solution.py:23
  479.1 23.7 %slice-start = ((s8[7864320]{0:T(1024)(128)(4,1)}), s8[4194304]{0:T(1024)(128)(4,1)S(1)}, s32[]{:S(2)}) async-start(s8[7864320]{0:T(1024)(128)(4,1)} %bitcast.355), calls=%async_computation.8 | async-start | bytes 8388608
  490.9 11.8 %slice-start.1 = ((s8[7864320]{0:T(1024)(128)(4,1)}), s8[3670016]{0:T(1024)(128)(4,1)S(1)}, s32[]{:S(2)}) async-start(s8[7864320]{0:T(1024)(128)(4,1)} %bitcast.355), calls=%async_computation.9 | async-start | bytes 7340032
  533.0 4.0 copy-start.4
  763.8 7.5 copy-start.1
Sparse Core Ops, SparseCore 0:
  24.0 33.0 reduce-scatter.1
